TPU v7x, 32 devices: a whole 2x2x4 slice. The times are simulated.
32 devices in a mesh: dp: 4 (over z), ep: 8 (over y, x, core).
Axes of the slice: x: 2, y: 2, z: 4, core: 2. Of those that a mesh axis runs over, the one named last changes fastest.
Arguments:
- tokens: bfloat16 [16384, 1024], P(('dp', 'ep')), may hold values from -6 to 6
- bucket: int32 [32], P(('dp', 'ep')), may hold values from 0 to 1
- expert_ids: int32 [16384, 1], P(('dp', 'ep')), may hold values from 0 to 7
- ln1_gain: float32 [1024], replicated, may hold values from 0.5 to 1.5
- qkv_weight: bfloat16 [1024, 3072], P('ep'), may hold values from -0.1875 to 0.1875
- out_weight: bfloat16 [1024, 1024], P('ep'), may hold values from -0.75 to 0.75
- ln2_gain: float32 [1024], replicated, may hold values from 0.5 to 1.5
- up_weight: bfloat16 [1024, 4096], P('ep'), may hold values from -0.1875 to 0.1875
- down_weight: bfloat16 [4096, 1024], P('ep'), may hold values from -0.1875 to 0.1875
- mix_weight: bfloat16 [1024, 2], replicated, may hold values from -0.1875 to 0.1875
- expert_up: bfloat16 [8, 1024, 4096], P('ep', None, 'dp'), may hold values from -0.1875 to 0.1875
- expert_down: bfloat16 [8, 4096, 1024], P('ep', 'dp'), may hold values from -0.1875 to 0.1875
- cotangent: bfloat16 [16384, 1024], P(('dp', 'ep')), may hold values from -6 to 6
Outputs:
- output: bfloat16 [16384, 1024], P(('dp', 'ep'))
- tokens_grad: float32 [16384, 1024], P(('dp', 'ep'))
- ln1_gain_grad: float32 [1024], replicated
- qkv_weight_grad: float32 [1024, 3072], P('ep')
- out_weight_grad: float32 [1024, 1024], P('ep')
- ln2_gain_grad: float32 [1024], replicated
- up_weight_grad: float32 [1024, 4096], P('ep')
- down_weight_grad: float32 [4096, 1024], P('ep')
- mix_weight_grad: float32 [1024, 2], replicated
- expert_up_grad: float32 [8, 1024, 4096], P('ep', None, 'dp')
- expert_down_grad: float32 [8, 4096, 1024], P('ep', 'dp')
All inputs are finite; a program needn't handle non-finite values.
Results may differ from a plain program's by a relative error of at most 0.02.
Values may be sent and summed in bfloat16 or wider, within the bound.
A program may use at most 320 MiB of HBM per device.

v0:
```python
import jax
import jax.numpy as jnp
from jax import lax
from jax.sharding import PartitionSpec as P

HEAD = 64
SHORT_SEQS = 4


def layer_norm(values_in, gain_vec):
    centred = values_in - jnp.mean(values_in, axis=-1, keepdims=True)
    inverse = lax.rsqrt(jnp.mean(centred * centred, axis=-1, keepdims=True) + 1e-05)
    return centred * inverse * gain_vec


def softmax_last(scores):
    row_peak = jnp.max(scores, axis=-1, keepdims=True)
    weights = jnp.exp(scores - row_peak)
    return weights / jnp.sum(weights, axis=-1, keepdims=True)


def gelu_backward(pre_act, act_grad):
    unused, pullback = jax.vjp(jax.nn.gelu, pre_act)
    return pullback(act_grad)[0]


def head_split(qkv_rows):
    length = qkv_rows.shape[0]
    width = qkv_rows.shape[1] // 3
    shaped = qkv_rows.reshape(length, 3, width // HEAD, HEAD)
    return (shaped[:, 0], shaped[:, 1], shaped[:, 2])


def masked_scores(query_rows, key_rows, allowed):
    scores = jnp.einsum(
        "qhd,khd->hqk", query_rows, key_rows, preferred_element_type=jnp.float32
    ) * HEAD ** (-0.5)
    return jnp.where(allowed[None], scores, -1e30)


def attention_forward(qkv_rows, allowed):
    length = qkv_rows.shape[0]
    query_rows, key_rows, value_rows = head_split(qkv_rows)
    scores = masked_scores(query_rows, key_rows, allowed)
    row_peak = jnp.max(scores, axis=-1, keepdims=True)
    weights = jnp.exp(scores - row_peak)
    totals = jnp.sum(weights, axis=-1, keepdims=True)
    prob_low = (weights / totals).astype(jnp.bfloat16)
    mixed_rows = jnp.einsum(
        "hqk,khd->qhd", prob_low, value_rows, preferred_element_type=jnp.float32
    )
    return (mixed_rows.reshape(length, -1).astype(jnp.bfloat16), row_peak + jnp.log(totals))


def attention_backward(qkv_rows, allowed, log_total, attended_grad):
    length = qkv_rows.shape[0]
    query_rows, key_rows, value_rows = head_split(qkv_rows)
    probs_full = jnp.exp(masked_scores(query_rows, key_rows, allowed) - log_total)
    grad_heads = attended_grad.reshape(query_rows.shape)
    prob_grad = jnp.einsum(
        "qhd,khd->hqk", grad_heads, value_rows, preferred_element_type=jnp.float32
    )
    centre = jnp.sum(probs_full * prob_grad, axis=-1, keepdims=True)
    score_grad = (probs_full * (prob_grad - centre)).astype(jnp.bfloat16)
    factor = HEAD ** (-0.5)
    query_grad = (
        jnp.einsum("hqk,khd->qhd", score_grad, key_rows, preferred_element_type=jnp.float32)
        * factor
    )
    key_grad = (
        jnp.einsum("hqk,qhd->khd", score_grad, query_rows, preferred_element_type=jnp.float32)
        * factor
    )
    value_grad = jnp.einsum(
        "hqk,qhd->khd",
        probs_full.astype(jnp.bfloat16),
        grad_heads,
        preferred_element_type=jnp.float32,
    )
    stacked = jnp.stack([query_grad, key_grad, value_grad], axis=1)
    return stacked.reshape(length, -1).astype(jnp.bfloat16)


def on_device(
    tokens,
    bucket,
    expert_ids,
    ln1_gain,
    qkv_weight,
    out_weight,
    ln2_gain,
    up_weight,
    down_weight,
    mix_weight,
    expert_up,
    expert_down,
    cotangent,
):
    length = tokens.shape[0]
    experts = lax.axis_size("ep") * expert_up.shape[0]
    capacity = 5 * length // (4 * experts)
    qkv_full, out_full, up_full, down_full = (
        lax.all_gather(qkv_weight, "ep", axis=0, tiled=True),
        lax.all_gather(out_weight, "ep", axis=0, tiled=True),
        lax.all_gather(up_weight, "ep", axis=0, tiled=True),
        lax.all_gather(down_weight, "ep", axis=0, tiled=True),
    )
    token_rows = tokens.astype(jnp.float32)
    normed_in = layer_norm(token_rows, ln1_gain).astype(jnp.bfloat16)
    qkv_rows = jnp.dot(normed_in, qkv_full, preferred_element_type=jnp.float32).astype(jnp.bfloat16)
    position = jnp.arange(length, dtype=jnp.int32)
    sequence = jnp.where(bucket[0] == 1, 0, position // (length // SHORT_SEQS))
    allowed = jnp.logical_and(
        sequence[:, None] == sequence[None, :], position[None, :] <= position[:, None]
    )
    attended, log_total = attention_forward(qkv_rows, allowed)
    attn_out = jnp.dot(attended, out_full, preferred_element_type=jnp.float32)
    hidden_res = token_rows + attn_out
    mid_low = layer_norm(hidden_res, ln2_gain).astype(jnp.bfloat16)
    dense_pre = jnp.dot(mid_low, up_full, preferred_element_type=jnp.float32)
    dense_act = jax.nn.gelu(dense_pre).astype(jnp.bfloat16)
    dense_out = jnp.dot(dense_act, down_full, preferred_element_type=jnp.float32)
    mixing = softmax_last(jnp.dot(mid_low, mix_weight, preferred_element_type=jnp.float32))
    chosen = expert_ids[:, 0]
    one_hot = (chosen[:, None] == jnp.arange(experts, dtype=jnp.int32)[None, :]).astype(jnp.int32)
    slot_index = jnp.sum(one_hot * (jnp.cumsum(one_hot, axis=0) - 1), axis=1)
    slot_match = (
        slot_index[:, None, None] == jnp.arange(capacity, dtype=jnp.int32)[None, None, :]
    ).astype(jnp.int32)
    table_flat = (
        (one_hot[:, :, None] * slot_match).reshape(length, experts * capacity).astype(jnp.bfloat16)
    )
    sent_rows = jnp.einsum(
        "tk,td->kd", table_flat, mid_low, preferred_element_type=jnp.float32
    ).astype(jnp.bfloat16)
    arrived = lax.all_to_all(
        sent_rows.reshape(experts, capacity, -1), "ep", split_axis=0, concat_axis=1, tiled=True
    )
    slot_rows = lax.all_gather(arrived, "dp", axis=1, tiled=True)
    expert_pre = jnp.einsum(
        "erd,edf->erf", slot_rows, expert_up, preferred_element_type=jnp.float32
    )
    expert_act = jax.nn.gelu(expert_pre).astype(jnp.bfloat16)
    partial_out = jnp.einsum(
        "erf,efd->erd", expert_act, expert_down, preferred_element_type=jnp.float32
    )
    summed_out = lax.psum_scatter(
        partial_out.astype(jnp.bfloat16), "dp", scatter_dimension=1, tiled=True
    )
    returned = lax.all_to_all(summed_out, "ep", split_axis=1, concat_axis=0, tiled=True)
    expert_out = jnp.dot(
        table_flat, returned.reshape(experts * capacity, -1), preferred_element_type=jnp.float32
    )
    result = hidden_res + mixing[:, 0:1] * dense_out + mixing[:, 1:2] * expert_out
    grad_out = cotangent.astype(jnp.float32)
    mix_grad = jnp.stack(
        [jnp.sum(grad_out * dense_out, axis=-1), jnp.sum(grad_out * expert_out, axis=-1)], axis=-1
    )
    logit_grad = (mixing * (mix_grad - jnp.sum(mixing * mix_grad, axis=-1, keepdims=True))).astype(
        jnp.bfloat16
    )
    mix_weight_grad = jnp.einsum(
        "td,tk->dk", mid_low, logit_grad, preferred_element_type=jnp.float32
    )
    dense_grad = (mixing[:, 0:1] * grad_out).astype(jnp.bfloat16)
    down_weight_grad = jnp.einsum(
        "tf,td->fd", dense_act, dense_grad, preferred_element_type=jnp.float32
    )
    dense_act_grad = jnp.einsum(
        "td,fd->tf", dense_grad, down_full, preferred_element_type=jnp.float32
    )
    dense_pre_grad = gelu_backward(dense_pre, dense_act_grad).astype(jnp.bfloat16)
    up_weight_grad = jnp.einsum(
        "td,tf->df", mid_low, dense_pre_grad, preferred_element_type=jnp.float32
    )
    mid_grad = jnp.einsum("tf,df->td", dense_pre_grad, up_full, preferred_element_type=jnp.float32)
    mid_grad = mid_grad + jnp.einsum(
        "tk,dk->td", logit_grad, mix_weight, preferred_element_type=jnp.float32
    )
    expert_grad = (mixing[:, 1:2] * grad_out).astype(jnp.bfloat16)
    sent_grad = jnp.einsum(
        "tk,td->kd", table_flat, expert_grad, preferred_element_type=jnp.float32
    ).astype(jnp.bfloat16)
    arrived_grad = lax.all_to_all(
        sent_grad.reshape(experts, capacity, -1), "ep", split_axis=0, concat_axis=1, tiled=True
    )
    slot_grad = lax.all_gather(arrived_grad, "dp", axis=1, tiled=True)
    expert_act_grad = jnp.einsum(
        "erd,efd->erf", slot_grad, expert_down, preferred_element_type=jnp.float32
    )
    expert_pre_grad = gelu_backward(expert_pre, expert_act_grad).astype(jnp.bfloat16)
    expert_down_grad = jnp.einsum(
        "erf,erd->efd", expert_act, slot_grad, preferred_element_type=jnp.float32
    )
    expert_up_grad = jnp.einsum(
        "erd,erf->edf", slot_rows, expert_pre_grad, preferred_element_type=jnp.float32
    )
    partial_in = jnp.einsum(
        "erf,edf->erd", expert_pre_grad, expert_up, preferred_element_type=jnp.float32
    )
    summed_in = lax.psum_scatter(
        partial_in.astype(jnp.bfloat16), "dp", scatter_dimension=1, tiled=True
    )
    back_rows = lax.all_to_all(summed_in, "ep", split_axis=1, concat_axis=0, tiled=True)
    mid_grad = mid_grad + jnp.dot(
        table_flat, back_rows.reshape(experts * capacity, -1), preferred_element_type=jnp.float32
    )
    unused_mid, mid_pull = jax.vjp(layer_norm, hidden_res, ln2_gain)
    res_part, ln2_gain_grad = mid_pull(mid_grad)
    res_grad = grad_out + res_part
    attn_out_grad = res_grad.astype(jnp.bfloat16)
    out_weight_grad = jnp.einsum(
        "td,te->de", attended, attn_out_grad, preferred_element_type=jnp.float32
    )
    attended_grad = jnp.einsum(
        "te,de->td", attn_out_grad, out_full, preferred_element_type=jnp.float32
    ).astype(jnp.bfloat16)
    qkv_grad = attention_backward(qkv_rows, allowed, log_total, attended_grad)
    qkv_weight_grad = jnp.einsum(
        "td,tk->dk", normed_in, qkv_grad, preferred_element_type=jnp.float32
    )
    normed_grad = jnp.einsum("tk,dk->td", qkv_grad, qkv_full, preferred_element_type=jnp.float32)
    unused_in, in_pull = jax.vjp(layer_norm, token_rows, ln1_gain)
    token_part, ln1_gain_grad = in_pull(normed_grad)
    tokens_grad = res_grad + token_part
    batch_sums = (
        lax.psum_scatter(
            qkv_weight_grad.astype(jnp.bfloat16), "ep", scatter_dimension=0, tiled=True
        ).astype(jnp.float32),
        lax.psum_scatter(
            out_weight_grad.astype(jnp.bfloat16), "ep", scatter_dimension=0, tiled=True
        ).astype(jnp.float32),
        lax.psum_scatter(
            up_weight_grad.astype(jnp.bfloat16), "ep", scatter_dimension=0, tiled=True
        ).astype(jnp.float32),
        lax.psum_scatter(
            down_weight_grad.astype(jnp.bfloat16), "ep", scatter_dimension=0, tiled=True
        ).astype(jnp.float32),
    )
    dense_shards = (
        lax.psum(batch_sums[0].astype(jnp.bfloat16), "dp").astype(jnp.float32),
        lax.psum(batch_sums[1].astype(jnp.bfloat16), "dp").astype(jnp.float32),
        lax.psum(batch_sums[2].astype(jnp.bfloat16), "dp").astype(jnp.float32),
        lax.psum(batch_sums[3].astype(jnp.bfloat16), "dp").astype(jnp.float32),
    )
    small_sums = lax.psum((ln1_gain_grad, ln2_gain_grad, mix_weight_grad), ("dp", "ep"))
    return (
        result.astype(jnp.bfloat16),
        tokens_grad,
        small_sums[0],
        dense_shards[0],
        dense_shards[1],
        small_sums[1],
        dense_shards[2],
        dense_shards[3],
        small_sums[2],
        expert_up_grad,
        expert_down_grad,
    )


def solution(mesh):
    placed = (
        P(("dp", "ep"), None),
        P(("dp", "ep")),
        P(("dp", "ep"), None),
        P(),
        P("ep", None),
        P("ep", None),
        P(),
        P("ep", None),
        P("ep", None),
        P(),
        P("ep", None, "dp"),
        P("ep", "dp", None),
        P(("dp", "ep"), None),
    )
    return jax.shard_map(
        on_device,
        mesh=mesh,
        in_specs=placed,
        out_specs=(
            P(("dp", "ep"), None),
            P(("dp", "ep"), None),
            P(),
            P("ep", None),
            P("ep", None),
            P(),
            P("ep", None),
            P("ep", None),
            P(),
            P("ep", None, "dp"),
            P("ep", "dp", None),
        ),
        check_vma=False,
    )
```

profile of v0, /device:TPU:0, one launch (start us, length us, event | category | flops | bytes accessed | tf_op | source)
XLA Modules:
  0.0 1117.8 jit_solution(12316198265122830779)
XLA Ops:
  17.8 40.4 %all-gather.7.cloned.1.call-done = bf16[1024,3072]{1,0:T(8,128)(2,1)} async-done(((bf16[128,3072]{1,0:T(8,128)(2,1)}), bf16[1024,3072]{1,0:T(8,128)(2,1)}) %all-gather.7.cloned.1.call-update) | async-done | bytes 6291472 | tf_op jit(solution)/shard_map/all_gather | solution.py:103
  105.2 21.3 %all_to_all.42 = bf16[8,80,1024]{2,1,0:T(8,128)(2,1)} all-to-all(bf16[8,80,1024]{2,1,0:T(8,128)(2,1)S(1)} %bitcast.156), channel_id=1, replica_groups=mesh['dp'=4,'ep'=8] {'ep'}, dimensions={0} | all-to-all | bytes 2621440 | tf_op jit(solution)/shard_map/all_to_all | solution.py:136
  126.5 97.3 %all-gather.15.cloned.1.call-done = bf16[1,2560,1024]{2,1,0:T(8,128)(2,1)} async-done(((bf16[1,640,1024]{2,1,0:T(8,128)(2,1)}), bf16[1,2560,1024]{2,1,0:T(8,128)(2,1)}) %all-gather.15.cloned.1.call-update) | async-done | bytes 5242896 | tf_op jit(solution)/shard_map/all_gather | solution.py:139
  246.3 90.7 %reduce-scatter.7.cloned.1.call-done = bf16[1,640,1024]{2,1,0:T(8,128)(2,1)} async-done(((bf16[1,2560,1024]{2,1,0:T(8,128)(2,1)}), bf16[1,640,1024]{2,1,0:T(8,128)(2,1)}) %reduce-scatter.7.cloned.1.call-update) | async-done | bytes 1310736 | tf_op jit(solution)/shard_map/reduce_scatter | solution.py:147
  342.3 10.7 reduce.2
  361.9 41.4 %all-gather.11.cloned.1.call-done = bf16[1024,4096]{1,0:T(8,128)(2,1)} async-done(((bf16[128,4096]{1,0:T(8,128)(2,1)}), bf16[1024,4096]{1,0:T(8,128)(2,1)}) %all-gather.11.cloned.1.call-update) | async-done | bytes 8388624 | tf_op jit(solution)/shard_map/all_gather | solution.py:105
  423.9 35.3 %all-gather.13.cloned.1.call-done = bf16[4096,1024]{1,0:T(8,128)(2,1)} async-done(((bf16[512,1024]{1,0:T(8,128)(2,1)}), bf16[4096,1024]{1,0:T(8,128)(2,1)}) %all-gather.13.cloned.1.call-update) | async-done | bytes 8388624 | tf_op jit(solution)/shard_map/all_gather | solution.py:106
  459.1 13.3 %fusion.49 = (f32[512]{0:T(512)S(1)}, f32[512]{0:T(512)S(1)}, f32[512,1024]{1,0:T(8,128)}) fusion(bf16[512,1024]{1,0:T(8,128)(2,1)} %param.25, f32[512,1024]{1,0:T(8,128)} %fusion.68, bf16[4096,1024]{1,0:T(8,128)(2,1)} %all-gather.13.cloned.1.call-done, f32[512,4096]{1,0:T(8,128)} %fusion.104), kind=kOutput, calls=%fused_computation.71 | convolution fusion | flops 4316462080 | bytes 22024192 | tf_op jit(solution)/shard_map/dot_general | solution.py:122
  473.5 21.3 %all_to_all.43 = bf16[8,80,1024]{2,1,0:T(8,128)(2,1)} all-to-all(bf16[8,80,1024]{2,1,0:T(8,128)(2,1)S(1)} %bitcast.157), channel_id=1, replica_groups=mesh['dp'=4,'ep'=8] {'ep'}, dimensions={0} | all-to-all | bytes 2621440 | tf_op jit(solution)/shard_map/all_to_all | solution.py:184
  495.1 97.0 %all-gather.17.cloned.1.call-done = bf16[1,2560,1024]{2,1,0:T(8,128)(2,1)} async-done(((bf16[1,640,1024]{2,1,0:T(8,128)(2,1)}), bf16[1,2560,1024]{2,1,0:T(8,128)(2,1)}) %all-gather.17.cloned.1.call-update) | async-done | bytes 5242896 | tf_op jit(solution)/shard_map/all_gather | solution.py:187
  592.1 14.9 %fusion.8 = bf16[2560,1024]{1,0:T(8,128)(2,1)S(1)} fusion(f32[2560,1024]{1,0:T(8,128)} %copy-done.41, bf16[1,2560,1024]{2,1,0:T(8,128)(2,1)} %all-gather.17.cloned.1.call-done, bf16[1,1024,1024]{2,1,0:T(8,128)(2,1)S(1)} %copy-done), kind=kOutput, calls=%fused_computation.18 | convolution fusion | flops 5421137920 | bytes 23068672 | tf_op jit(solution)/shard_map/erd,efd->erf/dot_general | solution.py:188
  629.0 12.5 %fusion.15 = bf16[512,4096]{1,0:T(8,128)(2,1)S(1)} fusion(f32[512,4096]{1,0:T(8,128)} %fusion.104, bf16[4096,1024]{1,0:T(8,128)(2,1)} %all-gather.13.cloned.1.call-done, bf16[512,1024]{1,0:T(8,128)(2,1)S(1)} %copy-done.13, f32[512]{0:T(512)S(1)} %bitcast.170), kind=kOutput, calls=%fused_computation.26 | convolution fusion | flops 4338483200 | bytes 22022144 | tf_op jit(solution)/shard_map/td,fd->tf/dot_general | solution.py:169
  652.9 56.6 %reduce-scatter.9.cloned.1.call-done = bf16[1,640,1024]{2,1,0:T(8,128)(2,1)} async-done(((bf16[1,2560,1024]{2,1,0:T(8,128)(2,1)}), bf16[1,640,1024]{2,1,0:T(8,128)(2,1)}) %reduce-scatter.9.cloned.1.call-update) | async-done | bytes 1310736 | tf_op jit(solution)/shard_map/reduce_scatter | solution.py:201
  730.3 10.6 fusion.105
  740.9 14.5 %all-to-all-done.3 = bf16[8,2,40960]{2,1,0:T(2,128)(2,1)} async-done(((bf16[8,2,40960]{2,1,0:T(2,128)(2,1)}), bf16[8,2,40960]{2,1,0:T(2,128)(2,1)}, u32[]{:S(2)}, u32[]{:S(2)}) %all-to-all-start.3) | async-done | bytes 1310752 | tf_op jit(solution)/shard_map/all_to_all | solution.py:204
  780.1 11.5 %multiply_reduce_fusion = (f32[16,512]{1,0:T(8,128)S(1)}, f32[16,512,512]{1,2,0:T(8,128)}) fusion(f32[16,512,512]{1,2,0:T(8,128)} %get-tuple-element.32, f32[16,512]{1,0:T(8,128)S(1)} %log_add_fusion, bf16[512,16,64]{0,2,1:T(8,128)(2,1)S(1)} %bitcast.144, bf16[512,3,16,64]{0,3,2,1:T(8,128)(2,1)} %bitcast.139), kind=kOutput, calls=%fused_computation.1 | convolution fusion | flops 549445632 | bytes 35717120 | tf_op jit(solution)/shard_map/qhd,khd->hqk/dot_general | solution.py:60
  791.6 12.9 %multiply_convert_fusion = bf16[16,512,512]{1,2,0:T(8,128)(2,1)S(1)} fusion(f32[16,512,512]{1,2,0:T(8,128)} %get-tuple-element.40, f32[16,512,512]{1,2,0:T(8,128)} %get-tuple-element.32, f32[16,512]{1,0:T(8,128)S(1)} %get-tuple-element.39, f32[16,512]{1,0:T(8,128)S(1)} %log_add_fusion), kind=kLoop, calls=%fused_computation | loop fusion | flops 16777216 | bytes 42008576 | tf_op jit(solution)/shard_map/convert_element_type | solution.py:64
  826.7 10.7 fusion.41
  837.4 28.6 %reduce-scatter.15.cloned.1.call-done = bf16[128,4096]{1,0:T(8,128)(2,1)} async-done(((bf16[1024,4096]{1,0:T(8,128)(2,1)}), bf16[128,4096]{1,0:T(8,128)(2,1)}) %reduce-scatter.15.cloned.1.call-update) | async-done | bytes 1048592 | tf_op jit(solution)/shard_map/reduce_scatter | solution.py:233
  866.0 45.1 %reduce-scatter.13.cloned.1.call-done = bf16[128,1024]{1,0:T(8,128)(2,1)} async-done(((bf16[1024,1024]{1,0:T(8,128)(2,1)}), bf16[128,1024]{1,0:T(8,128)(2,1)}) %reduce-scatter.13.cloned.1.call-update) | async-done | bytes 262160 | tf_op jit(solution)/shard_map/reduce_scatter | solution.py:230
  911.1 65.4 %reduce-scatter.11.cloned.1.call-done = bf16[128,3072]{1,0:T(8,128)(2,1)} async-done(((bf16[1024,3072]{1,0:T(8,128)(2,1)}), bf16[128,3072]{1,0:T(8,128)(2,1)}) %reduce-scatter.11.cloned.1.call-update) | async-done | bytes 786448 | tf_op jit(solution)/shard_map/reduce_scatter | solution.py:227
  976.5 11.6 %fusion.38 = f32[1,1024,1024]{2,1,0:T(8,128)} fusion(bf16[1,2560,1024]{2,1,0:T(8,128)(2,1)} %all-gather.17.cloned.1.call-done, f32[2560,1024]{1,0:T(8,128)} %copy-done.41), kind=kOutput, calls=%fused_computation.64 | convolution fusion | flops 5392302080 | bytes 19922944 | tf_op jit(solution)/shard_map/erf,erd->efd/dot_general | solution.py:192
  996.5 42.8 %all-reduce = (f32[1024]{0:T(1024)}, f32[1024]{0:T(1024)}, f32[1024,2]{0,1:T(2,128)}) all-reduce(f32[1024]{0:T(1024)S(1)} %get-tuple-element.13, f32[1024]{0:T(1024)S(1)} %get-tuple-element.11, f32[1024,2]{0,1:T(2,128)S(1)} %fusion.102), channel_id=1, replica_groups=mesh['dp'=4,'ep'=8] {'dp','ep'}, use_global_device_ids=true, to_apply=%region_22.23 | all-reduce | flops 4096 | bytes 32768 | tf_op jit(solution)/shard_map/psum | solution.py:246
  1043.8 58.4 %all-reduce.4.cloned.1.call-done = (bf16[128,3072]{1,0:T(8,128)(2,1)}, bf16[128,1024]{1,0:T(8,128)(2,1)}, bf16[128,4096]{1,0:T(8,128)(2,1)}, bf16[512,1024]{1,0:T(8,128)(2,1)}) async-done(((bf16[128,3072]{1,0:T(8,128)(2,1)}, bf16[128,1024]{1,0:T(8,128)(2,1)}, bf16[128,4096]{1,0:T(8,128)(2,1)}, bf16[512,1024]{1,0:T(8,128)(2,1)}), (bf16[128,3072]{1,0:T(8,128)(2,1)}, bf16[128,1024]{1,0:T(8,128)(2,1)}, ...) | async-done | bytes 3145744 | tf_op jit(solution)/shard_map/psum | solution.py:241
  (188 shorter events, 237.6 us)
Async XLA Ops:
  7.2 229.2 %copy-start = (bf16[1,1024,1024]{2,1,0:T(8,128)(2,1)S(1)}, bf16[1,1024,1024]{2,1,0:T(8,128)(2,1)}, u32[]{:S(2)}) copy-start(bf16[1,1024,1024]{2,1,0:T(8,128)(2,1)} %param.24) | copy-start | bytes 6291460
  7.2 51.0 %copy-start.5 = (bf16[512,1024]{1,0:T(8,128)(2,1)S(1)}, bf16[512,1024]{1,0:T(8,128)(2,1)}, u32[]{:S(2)}) copy-start(bf16[512,1024]{1,0:T(8,128)(2,1)} %param.13) | copy-start | bytes 3145732
  7.2 51.0 %copy-start.36 = (f32[1024]{0:T(1024)S(1)}, f32[1024]{0:T(1024)}, u32[]{:S(2)}) copy-start(f32[1024]{0:T(1024)} %param.16) | copy-start | bytes 12292
  7.2 51.0 %all-gather.7.cloned.1.call-start = ((), (), s32[]{:S(2)}) async-start(), calls=%async_computation.10 | async-start | bytes 7077888 | tf_op jit(solution)/shard_map/all_gather | solution.py:103
  8.0 91.4 %all-gather.9.cloned.1.call-start = ((), (), s32[]{:S(2)}) async-start(), calls=%async_computation.11 | async-start | bytes 2359296 | tf_op jit(solution)/shard_map/all_gather | solution.py:104
  8.7 215.1 %all-gather.15.cloned.1.call-start = ((), (), s32[]{:S(2)}) async-start(), calls=%async_computation.14 | async-start | bytes 6553600 | tf_op jit(solution)/shard_map/all_gather | solution.py:139
  10.9 55.1 %copy-start.26 = (f32[512]{0:T(512)}, f32[512]{0:T(512)S(1)}, u32[]{:S(2)}) copy-start(f32[512]{0:T(512)S(1)} %broadcast_multiply_fusion.1) | copy-start | bytes 6148
  12.5 53.4 %copy-start.30 = (f32[512]{0:T(512)}, f32[512]{0:T(512)S(1)}, u32[]{:S(2)}) copy-start(f32[512]{0:T(512)S(1)} %fusion.90) | copy-start | bytes 6148
  126.5 210.5 %reduce-scatter.7.cloned.1.call-start = ((), (), s32[]{:S(2)}) async-start(), calls=%async_computation.15 | async-start | bytes 6553600 | tf_op jit(solution)/shard_map/reduce_scatter | solution.py:147
  244.7 158.7 %all-gather.11.cloned.1.call-start = ((), (), s32[]{:S(2)}) async-start(), calls=%async_computation.12 | async-start | bytes 9437184 | tf_op jit(solution)/shard_map/all_gather | solution.py:105
  245.3 213.9 %all-gather.13.cloned.1.call-start = ((), (), s32[]{:S(2)}) async-start(), calls=%async_computation.13 | async-start | bytes 9437184 | tf_op jit(solution)/shard_map/all_gather | solution.py:106
  357.4 56.0 %all-to-all-start.1 = ((bf16[8,2,40960]{2,1,0:T(2,128)(2,1)}), bf16[8,2,40960]{2,1,0:T(2,128)(2,1)}, u32[]{:S(2)}, u32[]{:S(2)}) async-start(bf16[8,2,40960]{2,1,0:T(2,128)(2,1)} %reshape.349), calls=%async_computation.2 | async-start | bytes 2621440 | tf_op jit(solution)/shard_map/all_to_all | solution.py:150
  361.7 230.4 %all-gather.17.cloned.1.call-start = ((), (), s32[]{:S(2)}) async-start(), calls=%async_computation.16 | async-start | bytes 6553600 | tf_op jit(solution)/shard_map/all_gather | solution.py:187
  494.8 214.6 %reduce-scatter.9.cloned.1.call-start = ((), (), s32[]{:S(2)}) async-start(), calls=%async_computation.17 | async-start | bytes 6553600 | tf_op jit(solution)/shard_map/reduce_scatter | solution.py:201
  617.2 220.2 %reduce-scatter.17.cloned.1.call-start = ((), (), s32[]{:S(2)}) async-start(), calls=%async_computation.21 | async-start | bytes 9437184 | tf_op jit(solution)/shard_map/reduce_scatter | solution.py:236
  628.7 237.3 %reduce-scatter.15.cloned.1.call-start = ((), (), s32[]{:S(2)}) async-start(), calls=%async_computation.20 | async-start | bytes 9437184 | tf_op jit(solution)/shard_map/reduce_scatter | solution.py:233
  725.8 29.6 %all-to-all-start.3 = ((bf16[8,2,40960]{2,1,0:T(2,128)(2,1)}), bf16[8,2,40960]{2,1,0:T(2,128)(2,1)}, u32[]{:S(2)}, u32[]{:S(2)}) async-start(bf16[8,2,40960]{2,1,0:T(2,128)(2,1)} %reshape.351), calls=%async_computation.5 | async-start | bytes 2621440 | tf_op jit(solution)/shard_map/all_to_all | solution.py:204
  730.1 31.5 %copy-start.23 = (f32[512]{0:T(512)S(1)}, f32[512]{0:T(512)}, u32[]{:S(2)}) copy-start(f32[512]{0:T(512)} %copy-done.22) | copy-start | bytes 6148
  730.1 31.5 %copy-start.25 = (f32[1024]{0:T(1024)S(1)}, f32[1024]{0:T(1024)}, u32[]{:S(2)}) copy-start(f32[1024]{0:T(1024)} %param.19) | copy-start | bytes 12292
  730.1 31.5 %copy-start.29 = (f32[512]{0:T(512)S(1)}, f32[512]{0:T(512)}, u32[]{:S(2)}) copy-start(f32[512]{0:T(512)} %copy-done.28) | copy-start | bytes 6148
  730.1 181.0 %reduce-scatter.13.cloned.1.call-start = ((), (), s32[]{:S(2)}) async-start(), calls=%async_computation.19 | async-start | bytes 2359296 | tf_op jit(solution)/shard_map/reduce_scatter | solution.py:230
  779.8 196.7 %reduce-scatter.11.cloned.1.call-start = ((), (), s32[]{:S(2)}) async-start(), calls=%async_computation.18 | async-start | bytes 7077888 | tf_op jit(solution)/shard_map/reduce_scatter | solution.py:227
  826.1 276.0 %all-reduce.4.cloned.1.call-start = ((), (), s32[]{:S(2)}) async-start(), calls=%async_computation.22 | async-start | bytes 6291456 | tf_op jit(solution)/shard_map/psum | solution.py:241
  988.1 51.2 %copy-start.15 = (bf16[512,1024]{1,0:T(8,128)(2,1)S(1)}, bf16[512,1024]{1,0:T(8,128)(2,1)}, u32[]{:S(2)}) copy-start(bf16[512,1024]{1,0:T(8,128)(2,1)} %param.25) | copy-start | bytes 3145732
  (34 other events, 212.8 us)
Sparse Core Ops, SparseCore 0:
  9.9 48.2 all-gather.6
  60.1 27.8 all-gather.8
  126.6 97.1 all-gather.14
  244.8 92.1 reduce-scatter.6
  338.7 64.6 all-gather.10
  405.1 53.9 all-gather.12
  494.9 97.1 all-gather.16
  617.3 92.1 reduce-scatter.8
  712.9 78.0 reduce-scatter.16
  794.7 71.2 reduce-scatter.14
  869.9 41.1 reduce-scatter.12
  914.7 61.7 reduce-scatter.10
  979.1 123.0 all-reduce.3
where the time goes:
time: 1120 us
  waiting for transfers between devices  673 us (60%)
  matrix products  214 us (19%)
  blocking collectives  85.4 us (8%)
  other arithmetic  67 us (6%)
  local copies, waits for them, and re-layouts  52 us (5%)
  between operations  15.4 us (1%)
    all_gather x1, waiting for transfers between devices, on_device(): slot_rows = lax.all_gather(arrived, 'dp', axis=1, tiled=True)  97.3 us
    all_gather x1, waiting for transfers between devices, on_device(): slot_grad = lax.all_gather(arrived_grad, 'dp', axis=1, tiled=True)  97 us
    reduce_scatter x1, waiting for transfers between devices, on_device(): lax.psum_scatter(partial_out.astype(jnp.bfloat16), 'dp', scatter_dimensio...  90.7 us
    reduce_scatter x1, waiting for transfers between devices, on_device(): lax.psum_scatter(qkv_weight_grad.astype(jnp.bfloat16), 'ep', scatter_dime...  65.4 us
    psum x1, waiting for transfers between devices, on_device(): lax.psum(batch_sums[0].astype(jnp.bfloat16), 'dp').astype(jnp.float32)  58.4 us
    reduce_scatter x1, waiting for transfers between devices, on_device(): lax.psum_scatter(partial_in.astype(jnp.bfloat16), 'dp', scatter_dimension...  56.6 us
    reduce_scatter x1, waiting for transfers between devices, on_device(): lax.psum_scatter(out_weight_grad.astype(jnp.bfloat16), 'ep', scatter_dime...  45.1 us
    psum x1, blocking collectives, on_device(): lax.psum((ln1_gain_grad, ln2_gain_grad, mix_weight_grad), ('dp', 'ep'))  42.8 us
  transfers between devices with their start and end apart: 15, of which 12 were waited for; matrix products, arithmetic and copies ran while one was open for 22% of the time, Pallas kernels for 0%

commit v1 on v0

--- a/solution.py
+++ b/solution.py
@@ -237,8 +237,13 @@
             down_weight_grad.astype(jnp.bfloat16), "ep", scatter_dimension=0, tiled=True
         ).astype(jnp.float32),
     )
+
+    def trails_draft(local_x, chip_axis):
+        block_out = lax.all_gather(local_x, chip_axis)
+        return jnp.sum(block_out, 0)
+
     dense_shards = (
-        lax.psum(batch_sums[0].astype(jnp.bfloat16), "dp").astype(jnp.float32),
+        trails_draft(batch_sums[0].astype(jnp.bfloat16), "dp").astype(jnp.float32),
         lax.psum(batch_sums[1].astype(jnp.bfloat16), "dp").astype(jnp.float32),
         lax.psum(batch_sums[2].astype(jnp.bfloat16), "dp").astype(jnp.float32),
         lax.psum(batch_sums[3].astype(jnp.bfloat16), "dp").astype(jnp.float32),

time: 1120 us -> 1150 us (1.027)
  waiting for transfers between devices: 673 us -> 707 us
    all_gather x0 -> x1, waiting for transfers between devices: none -> 57.7 us  [trails_draft(): block_out = lax.all_gather(local_x, chip_axis)]
    psum x1, waiting for transfers between devices: 58.4 us -> 23.9 us  [on_device(): lax.psum(batch_sums[1].astype(jnp.bfloat16), 'dp').astype(jnp.float32)]
  transfers between devices with their start and end apart: 15 -> 16, of which waited for: 12 -> 13; matrix products, arithmetic and copies ran while one was open for 22% -> 22% of each run, Pallas kernels for 0% -> 0%
where the time goes in v1:
time: 1150 us
  waiting for transfers between devices  707 us (61%)
  matrix products  214 us (19%)
  blocking collectives  82.9 us (7%)
  other arithmetic  68.3 us (6%)
  local copies, waits for them, and re-layouts  52 us (5%)
  between operations  15.4 us (1%)
    all_gather x1, waiting for transfers between devices, on_device(): slot_rows = lax.all_gather(arrived, 'dp', axis=1, tiled=True)  97.3 us
    all_gather x1, waiting for transfers between devices, on_device(): slot_grad = lax.all_gather(arrived_grad, 'dp', axis=1, tiled=True)  97 us
    reduce_scatter x1, waiting for transfers between devices, on_device(): lax.psum_scatter(partial_out.astype(jnp.bfloat16), 'dp', scatter_dimensio...  90.7 us
    reduce_scatter x1, waiting for transfers between devices, on_device(): lax.psum_scatter(qkv_weight_grad.astype(jnp.bfloat16), 'ep', scatter_dime...  64.8 us
    all_gather x1, waiting for transfers between devices, trails_draft(): block_out = lax.all_gather(local_x, chip_axis)  57.7 us
    reduce_scatter x1, waiting for transfers between devices, on_device(): lax.psum_scatter(partial_in.astype(jnp.bfloat16), 'dp', scatter_dimension...  56.6 us
    reduce_scatter x1, waiting for transfers between devices, on_device(): lax.psum_scatter(out_weight_grad.astype(jnp.bfloat16), 'ep', scatter_dime...  45.1 us
    all_gather x1, waiting for transfers between devices, on_device(): lax.all_gather(up_weight, 'ep', axis=0, tiled=True)  41.4 us
  transfers between devices with their start and end apart: 16, of which 13 were waited for; matrix products, arithmetic and copies ran while one was open for 22% of the time, Pallas kernels for 0%

profile of v1, /device:TPU:0, one launch (start us, length us, event | category | flops | bytes accessed | tf_op | source)
XLA Modules:
  0.0 1150.2 jit_solution(11915806450656047086)
XLA Ops:
  17.8 40.4 %all-gather.9.cloned.1.call-done = bf16[1024,3072]{1,0:T(8,128)(2,1)} async-done(((bf16[128,3072]{1,0:T(8,128)(2,1)}), bf16[1024,3072]{1,0:T(8,128)(2,1)}) %all-gather.9.cloned.1.call-update) | async-done | bytes 6291472 | tf_op jit(solution)/shard_map/all_gather | solution.py:103
  105.2 21.3 %all_to_all.42 = bf16[8,80,1024]{2,1,0:T(8,128)(2,1)} all-to-all(bf16[8,80,1024]{2,1,0:T(8,128)(2,1)S(1)} %bitcast.158), channel_id=1, replica_groups=mesh['dp'=4,'ep'=8] {'ep'}, dimensions={0} | all-to-all | bytes 2621440 | tf_op jit(solution)/shard_map/all_to_all | solution.py:136
  126.5 97.3 %all-gather.17.cloned.1.call-done = bf16[1,2560,1024]{2,1,0:T(8,128)(2,1)} async-done(((bf16[1,640,1024]{2,1,0:T(8,128)(2,1)}), bf16[1,2560,1024]{2,1,0:T(8,128)(2,1)}) %all-gather.17.cloned.1.call-update) | async-done | bytes 5242896 | tf_op jit(solution)/shard_map/all_gather | solution.py:139
  246.3 90.7 %reduce-scatter.7.cloned.1.call-done = bf16[1,640,1024]{2,1,0:T(8,128)(2,1)} async-done(((bf16[1,2560,1024]{2,1,0:T(8,128)(2,1)}), bf16[1,640,1024]{2,1,0:T(8,128)(2,1)}) %reduce-scatter.7.cloned.1.call-update) | async-done | bytes 1310736 | tf_op jit(solution)/shard_map/reduce_scatter | solution.py:147
  342.3 10.7 reduce.3
  361.9 41.4 %all-gather.13.cloned.1.call-done = bf16[1024,4096]{1,0:T(8,128)(2,1)} async-done(((bf16[128,4096]{1,0:T(8,128)(2,1)}), bf16[1024,4096]{1,0:T(8,128)(2,1)}) %all-gather.13.cloned.1.call-update) | async-done | bytes 8388624 | tf_op jit(solution)/shard_map/all_gather | solution.py:105
  423.9 35.3 %all-gather.15.cloned.1.call-done = bf16[4096,1024]{1,0:T(8,128)(2,1)} async-done(((bf16[512,1024]{1,0:T(8,128)(2,1)}), bf16[4096,1024]{1,0:T(8,128)(2,1)}) %all-gather.15.cloned.1.call-update) | async-done | bytes 8388624 | tf_op jit(solution)/shard_map/all_gather | solution.py:106
  459.1 13.3 %fusion.49 = (f32[512]{0:T(512)S(1)}, f32[512]{0:T(512)S(1)}, f32[512,1024]{1,0:T(8,128)}) fusion(bf16[512,1024]{1,0:T(8,128)(2,1)} %param.25, f32[512,1024]{1,0:T(8,128)} %fusion.68, bf16[4096,1024]{1,0:T(8,128)(2,1)} %all-gather.15.cloned.1.call-done, f32[512,4096]{1,0:T(8,128)} %fusion.104), kind=kOutput, calls=%fused_computation.71 | convolution fusion | flops 4316462080 | bytes 22024192 | tf_op jit(solution)/shard_map/dot_general | solution.py:122
  473.5 21.3 %all_to_all.43 = bf16[8,80,1024]{2,1,0:T(8,128)(2,1)} all-to-all(bf16[8,80,1024]{2,1,0:T(8,128)(2,1)S(1)} %bitcast.159), channel_id=1, replica_groups=mesh['dp'=4,'ep'=8] {'ep'}, dimensions={0} | all-to-all | bytes 2621440 | tf_op jit(solution)/shard_map/all_to_all | solution.py:184
  495.1 97.0 %all-gather.19.cloned.1.call-done = bf16[1,2560,1024]{2,1,0:T(8,128)(2,1)} async-done(((bf16[1,640,1024]{2,1,0:T(8,128)(2,1)}), bf16[1,2560,1024]{2,1,0:T(8,128)(2,1)}) %all-gather.19.cloned.1.call-update) | async-done | bytes 5242896 | tf_op jit(solution)/shard_map/all_gather | solution.py:187
  592.1 14.9 %fusion.8 = bf16[2560,1024]{1,0:T(8,128)(2,1)S(1)} fusion(f32[2560,1024]{1,0:T(8,128)} %copy-done.41, bf16[1,2560,1024]{2,1,0:T(8,128)(2,1)} %all-gather.19.cloned.1.call-done, bf16[1,1024,1024]{2,1,0:T(8,128)(2,1)S(1)} %copy-done), kind=kOutput, calls=%fused_computation.18 | convolution fusion | flops 5421137920 | bytes 23068672 | tf_op jit(solution)/shard_map/erd,efd->erf/dot_general | solution.py:188
  629.0 12.5 %fusion.15 = bf16[512,4096]{1,0:T(8,128)(2,1)S(1)} fusion(f32[512,4096]{1,0:T(8,128)} %fusion.104, bf16[4096,1024]{1,0:T(8,128)(2,1)} %all-gather.15.cloned.1.call-done, bf16[512,1024]{1,0:T(8,128)(2,1)S(1)} %copy-done.13, f32[512]{0:T(512)S(1)} %bitcast.172), kind=kOutput, calls=%fused_computation.26 | convolution fusion | flops 4338483200 | bytes 22022144 | tf_op jit(solution)/shard_map/td,fd->tf/dot_general | solution.py:169
  652.9 56.6 %reduce-scatter.9.cloned.1.call-done = bf16[1,640,1024]{2,1,0:T(8,128)(2,1)} async-done(((bf16[1,2560,1024]{2,1,0:T(8,128)(2,1)}), bf16[1,640,1024]{2,1,0:T(8,128)(2,1)}) %reduce-scatter.9.cloned.1.call-update) | async-done | bytes 1310736 | tf_op jit(solution)/shard_map/reduce_scatter | solution.py:201
  730.3 10.6 fusion.105
  740.9 14.5 %all-to-all-done.3 = bf16[8,2,40960]{2,1,0:T(2,128)(2,1)} async-done(((bf16[8,2,40960]{2,1,0:T(2,128)(2,1)}), bf16[8,2,40960]{2,1,0:T(2,128)(2,1)}, u32[]{:S(2)}, u32[]{:S(2)}) %all-to-all-start.3) | async-done | bytes 1310752 | tf_op jit(solution)/shard_map/all_to_all | solution.py:204
  780.1 11.5 %multiply_reduce_fusion = (f32[16,512]{1,0:T(8,128)S(1)}, f32[16,512,512]{1,2,0:T(8,128)}) fusion(f32[16,512,512]{1,2,0:T(8,128)} %get-tuple-element.31, f32[16,512]{1,0:T(8,128)S(1)} %log_add_fusion, bf16[512,16,64]{0,2,1:T(8,128)(2,1)S(1)} %bitcast.145, bf16[512,3,16,64]{0,3,2,1:T(8,128)(2,1)} %bitcast.140), kind=kOutput, calls=%fused_computation.1 | convolution fusion | flops 549445632 | bytes 35717120 | tf_op jit(solution)/shard_map/qhd,khd->hqk/dot_general | solution.py:60
  791.6 12.9 %multiply_convert_fusion = bf16[16,512,512]{1,2,0:T(8,128)(2,1)S(1)} fusion(f32[16,512,512]{1,2,0:T(8,128)} %get-tuple-element.39, f32[16,512,512]{1,2,0:T(8,128)} %get-tuple-element.31, f32[16,512]{1,0:T(8,128)S(1)} %get-tuple-element.38, f32[16,512]{1,0:T(8,128)S(1)} %log_add_fusion), kind=kLoop, calls=%fused_computation | loop fusion | flops 16777216 | bytes 42008576 | tf_op jit(solution)/shard_map/convert_element_type | solution.py:64
  826.2 39.8 %reduce-scatter.15.cloned.1.call-done = bf16[128,4096]{1,0:T(8,128)(2,1)} async-done(((bf16[1024,4096]{1,0:T(8,128)(2,1)}), bf16[128,4096]{1,0:T(8,128)(2,1)}) %reduce-scatter.15.cloned.1.call-update) | async-done | bytes 1048592 | tf_op jit(solution)/shard_map/reduce_scatter | solution.py:233
  866.0 45.1 %reduce-scatter.13.cloned.1.call-done = bf16[128,1024]{1,0:T(8,128)(2,1)} async-done(((bf16[1024,1024]{1,0:T(8,128)(2,1)}), bf16[128,1024]{1,0:T(8,128)(2,1)}) %reduce-scatter.13.cloned.1.call-update) | async-done | bytes 262160 | tf_op jit(solution)/shard_map/reduce_scatter | solution.py:230
  911.7 64.8 %reduce-scatter.11.cloned.1.call-done = bf16[128,3072]{1,0:T(8,128)(2,1)} async-done(((bf16[1024,3072]{1,0:T(8,128)(2,1)}), bf16[128,3072]{1,0:T(8,128)(2,1)}) %reduce-scatter.11.cloned.1.call-update) | async-done | bytes 786448 | tf_op jit(solution)/shard_map/reduce_scatter | solution.py:227
  976.5 11.4 fusion.38
  1006.9 40.3 %all-reduce = (f32[1024]{0:T(1024)}, f32[1024]{0:T(1024)}, f32[1024,2]{0,1:T(2,128)}) all-reduce(f32[1024]{0:T(1024)S(1)} %get-tuple-element.13, f32[1024]{0:T(1024)S(1)} %get-tuple-element.11, f32[1024,2]{0,1:T(2,128)S(1)} %fusion.102), channel_id=1, replica_groups=mesh['dp'=4,'ep'=8] {'dp','ep'}, use_global_device_ids=true, to_apply=%region_22.23 | all-reduce | flops 4096 | bytes 32768 | tf_op jit(solution)/shard_map/psum | solution.py:251
  1051.7 23.9 %all-reduce.4.cloned.1.call-done = (bf16[128,1024]{1,0:T(8,128)(2,1)}, bf16[128,4096]{1,0:T(8,128)(2,1)}, bf16[512,1024]{1,0:T(8,128)(2,1)}) async-done(((bf16[128,1024]{1,0:T(8,128)(2,1)}, bf16[128,4096]{1,0:T(8,128)(2,1)}, bf16[512,1024]{1,0:T(8,128)(2,1)}), (bf16[128,1024]{1,0:T(8,128)(2,1)}, bf16[128,4096]{1,0:T(8,128)(2,1)}, bf16[512,1024]{1,0:T(8,128)(2,1)})) %all-reduce.4.cloned.1.call-update) | async-done | bytes 2359312 | tf_op jit(solution)/shard_map/psum | solution.py:247
  1081.9 57.7 %all-gather.21.cloned.1.call-done = bf16[512,3072]{1,0:T(8,128)(2,1)} async-done(((bf16[128,3072]{1,0:T(8,128)(2,1)}), bf16[512,3072]{1,0:T(8,128)(2,1)}) %all-gather.21.cloned.1.call-update) | async-done | bytes 3145744 | tf_op jit(solution)/shard_map/all_gather | solution.py:242
  (192 shorter events, 249.5 us)
Async XLA Ops:
  7.2 229.2 %copy-start = (bf16[1,1024,1024]{2,1,0:T(8,128)(2,1)S(1)}, bf16[1,1024,1024]{2,1,0:T(8,128)(2,1)}, u32[]{:S(2)}) copy-start(bf16[1,1024,1024]{2,1,0:T(8,128)(2,1)} %param.24) | copy-start | bytes 6291460
  7.2 51.0 %copy-start.5 = (bf16[512,1024]{1,0:T(8,128)(2,1)S(1)}, bf16[512,1024]{1,0:T(8,128)(2,1)}, u32[]{:S(2)}) copy-start(bf16[512,1024]{1,0:T(8,128)(2,1)} %param.13) | copy-start | bytes 3145732
  7.2 51.0 %copy-start.36 = (f32[1024]{0:T(1024)S(1)}, f32[1024]{0:T(1024)}, u32[]{:S(2)}) copy-start(f32[1024]{0:T(1024)} %param.16) | copy-start | bytes 12292
  7.2 51.0 %all-gather.9.cloned.1.call-start = ((), (), s32[]{:S(2)}) async-start(), calls=%async_computation.10 | async-start | bytes 7077888 | tf_op jit(solution)/shard_map/all_gather | solution.py:103
  8.0 91.4 %all-gather.11.cloned.1.call-start = ((), (), s32[]{:S(2)}) async-start(), calls=%async_computation.11 | async-start | bytes 2359296 | tf_op jit(solution)/shard_map/all_gather | solution.py:104
  8.7 215.1 %all-gather.17.cloned.1.call-start = ((), (), s32[]{:S(2)}) async-start(), calls=%async_computation.14 | async-start | bytes 6553600 | tf_op jit(solution)/shard_map/all_gather | solution.py:139
  10.9 55.1 %copy-start.26 = (f32[512]{0:T(512)}, f32[512]{0:T(512)S(1)}, u32[]{:S(2)}) copy-start(f32[512]{0:T(512)S(1)} %broadcast_multiply_fusion.1) | copy-start | bytes 6148
  12.5 53.4 %copy-start.30 = (f32[512]{0:T(512)}, f32[512]{0:T(512)S(1)}, u32[]{:S(2)}) copy-start(f32[512]{0:T(512)S(1)} %fusion.90) | copy-start | bytes 6148
  126.5 210.5 %reduce-scatter.7.cloned.1.call-start = ((), (), s32[]{:S(2)}) async-start(), calls=%async_computation.15 | async-start | bytes 6553600 | tf_op jit(solution)/shard_map/reduce_scatter | solution.py:147
  244.7 158.7 %all-gather.13.cloned.1.call-start = ((), (), s32[]{:S(2)}) async-start(), calls=%async_computation.12 | async-start | bytes 9437184 | tf_op jit(solution)/shard_map/all_gather | solution.py:105
  245.3 213.9 %all-gather.15.cloned.1.call-start = ((), (), s32[]{:S(2)}) async-start(), calls=%async_computation.13 | async-start | bytes 9437184 | tf_op jit(solution)/shard_map/all_gather | solution.py:106
  357.4 56.0 %all-to-all-start.1 = ((bf16[8,2,40960]{2,1,0:T(2,128)(2,1)}), bf16[8,2,40960]{2,1,0:T(2,128)(2,1)}, u32[]{:S(2)}, u32[]{:S(2)}) async-start(bf16[8,2,40960]{2,1,0:T(2,128)(2,1)} %reshape.350), calls=%async_computation.2 | async-start | bytes 2621440 | tf_op jit(solution)/shard_map/all_to_all | solution.py:150
  361.7 230.4 %all-gather.19.cloned.1.call-start = ((), (), s32[]{:S(2)}) async-start(), calls=%async_computation.16 | async-start | bytes 6553600 | tf_op jit(solution)/shard_map/all_gather | solution.py:187
  494.8 214.6 %reduce-scatter.9.cloned.1.call-start = ((), (), s32[]{:S(2)}) async-start(), calls=%async_computation.17 | async-start | bytes 6553600 | tf_op jit(solution)/shard_map/reduce_scatter | solution.py:201
  617.2 209.1 %reduce-scatter.17.cloned.1.call-start = ((), (), s32[]{:S(2)}) async-start(), calls=%async_computation.21 | async-start | bytes 9437184 | tf_op jit(solution)/shard_map/reduce_scatter | solution.py:236
  628.7 237.3 %reduce-scatter.15.cloned.1.call-start = ((), (), s32[]{:S(2)}) async-start(), calls=%async_computation.20 | async-start | bytes 9437184 | tf_op jit(solution)/shard_map/reduce_scatter | solution.py:233
  725.8 29.6 %all-to-all-start.3 = ((bf16[8,2,40960]{2,1,0:T(2,128)(2,1)}), bf16[8,2,40960]{2,1,0:T(2,128)(2,1)}, u32[]{:S(2)}, u32[]{:S(2)}) async-start(bf16[8,2,40960]{2,1,0:T(2,128)(2,1)} %reshape.352), calls=%async_computation.5 | async-start | bytes 2621440 | tf_op jit(solution)/shard_map/all_to_all | solution.py:204
  730.1 31.5 %copy-start.23 = (f32[512]{0:T(512)S(1)}, f32[512]{0:T(512)}, u32[]{:S(2)}) copy-start(f32[512]{0:T(512)} %copy-done.22) | copy-start | bytes 6148
  730.1 181.0 %reduce-scatter.13.cloned.1.call-start = ((), (), s32[]{:S(2)}) async-start(), calls=%async_computation.19 | async-start | bytes 2359296 | tf_op jit(solution)/shard_map/reduce_scatter | solution.py:230
  779.8 196.7 %reduce-scatter.11.cloned.1.call-start = ((), (), s32[]{:S(2)}) async-start(), calls=%async_computation.18 | async-start | bytes 7077888 | tf_op jit(solution)/shard_map/reduce_scatter | solution.py:227
  826.1 249.5 %all-reduce.4.cloned.1.call-start = ((), (), s32[]{:S(2)}) async-start(), calls=%async_computation.23 | async-start | bytes 4718592 | tf_op jit(solution)/shard_map/psum | solution.py:247
  911.1 228.4 %all-gather.21.cloned.1.call-start = ((), (), s32[]{:S(2)}) async-start(), calls=%async_computation.22 | async-start | bytes 3932160 | tf_op jit(solution)/shard_map/all_gather | solution.py:242
  998.5 48.7 %copy-start.15 = (bf16[512,1024]{1,0:T(8,128)(2,1)S(1)}, bf16[512,1024]{1,0:T(8,128)(2,1)}, u32[]{:S(2)}) copy-start(bf16[512,1024]{1,0:T(8,128)(2,1)} %param.25) | copy-start | bytes 3145732
  1080.3 63.1 %copy-start.1 = (bf16[1,1024,1024]{2,1,0:T(8,128)(2,1)S(1)}, bf16[1,1024,1024]{2,1,0:T(8,128)(2,1)}, u32[]{:S(2)}) copy-start(bf16[1,1024,1024]{2,1,0:T(8,128)(2,1)} %param.24) | copy-start | bytes 6291460
  (35 other events, 265.2 us)
Sparse Core Ops, SparseCore 0:
  9.9 48.2 all-gather.8
  60.1 27.8 all-gather.10
  126.6 97.1 all-gather.16
  244.8 92.1 reduce-scatter.6
  338.7 64.6 all-gather.12
  405.1 53.9 all-gather.14
  494.9 97.1 all-gather.18
  617.3 92.1 reduce-scatter.8
  712.9 78.0 reduce-scatter.16
  794.7 71.2 reduce-scatter.14
  869.9 41.1 reduce-scatter.12
  914.7 61.7 reduce-scatter.10
  979.1 96.5 all-reduce.3
  1077.1 62.4 all-gather.20
